TPU v7x, 128 devices: a whole 4x4x4 slice. The times are simulated.
128 devices in a mesh: gx: 8 (over z, core), gy: 16 (over x, y).
Axes of the slice: x: 4, y: 4, z: 4, core: 2. Of those that a mesh axis runs over, the one named last changes fastest.
Arguments:
- state: float32 [100, 524288], P(None, ('gx', 'gy')), may hold values from -6 to 6
- adjoint: float32 [175, 524288], P(None, ('gx', 'gy')), may hold values from -6 to 6
- geometry: float32 [60, 524288], P(None, ('gx', 'gy')), may hold values from -6 to 6
- face_blocks: float32 [75, 1048576], P(None, ('gx', 'gy')), may hold values from -6 to 6
- face_elem: int32 [1048576], P(('gx', 'gy')), may hold values from 0 to 4095, as said below
- move_ids: int32 [512, 1024], P(('gx', 'gy')), may hold values from 0 to 4095, as said below
- move_counts: int32 [512], P(('gx', 'gy')), may hold values from 0 to 1024, as said below
- basis: float32 [46, 20], replicated, may hold values from -1.25 to 1.25
- geo_grad: float32 [3, 46, 20], replicated, may hold values from -1.25 to 1.25
- test_grad: float32 [35, 138], replicated, may hold values from -0.5 to 0.5
- lift: float32 [35, 15], replicated, may hold values from -1.5 to 1.5
- speeds: float32 [3, 5], replicated, may hold values from -1 to 1
Outputs:
- state_out: float32 [100, 1048576], P(None, ('gx', 'gy'))
- adjoint_out: float32 [175, 1048576], P(None, ('gx', 'gy'))
- geometry_out: float32 [60, 1048576], P(None, ('gx', 'gy'))
- faces_out: float32 [75, 2097152], P(None, ('gx', 'gy'))
- residual: float32 [175, 524288], P(None, ('gx', 'gy'))
Inputs may be any that keep to these rules, and one draw needn't show every extreme that they name: `move_counts`: entry 4 d + k is how many elements device d sends toward its side k; it is 0 toward a side with no device, and every device sends exactly 1024 elements toward one side. `move_ids`: row 4 d + k lists device d's local element numbers for side k, the first move_counts[4 d + k] of them used; the 4096 numbers of one device are distinct. `face_elem`: every element of a device owns exactly two of the device's faces.
All inputs are finite; a program needn't handle non-finite values.
Results may differ from a plain program's by a relative error of at most 0.0003.
Values sent between devices are 32-bit elements; how exact they have to be, the bound alone decides.
No kernel may reach another device: no remote copies, remote signals or barrier semaphores. Data moves between devices by JAX's collectives and lax.ppermute only.
A program may use at most 128 MiB of HBM per device.

v0:
```python
import jax
import jax.numpy as jnp
from jax import lax
from jax.sharding import PartitionSpec as P


def with_halo(value, sides, width):
    for axis, dim in sides:
        size, length = (lax.axis_size(axis), value.shape[dim])
        up = [(i, (i + 1) % size) for i in range(size - 1)]
        down = [(j, i) for i, j in up]
        last = lax.slice_in_dim(value, length - width, length, axis=dim)
        initial = lax.slice_in_dim(value, 0, width, axis=dim)
        before = lax.ppermute(last, axis, up)
        after = lax.ppermute(initial, axis, down)
        value = jnp.concatenate([before, value, after], axis=dim)
    return value


def departures(ids, counts, elems):
    cap = ids.shape[1]
    live = (jnp.arange(cap, dtype=jnp.int32)[None, :] < counts[:, None]).astype(jnp.float32)
    departed = jnp.zeros((elems,), jnp.float32).at[ids.reshape(-1)].max(live.reshape(-1))
    return (live, 1.0 - departed)


def face_numbers(owners, elems):
    nfaces = owners.shape[0]
    where = jnp.arange(nfaces, dtype=jnp.int32)
    first = jnp.full((elems,), nfaces, jnp.int32).at[owners].min(where)
    second = jnp.zeros((elems,), jnp.int32).at[owners].max(where)
    return (first, second)


def enriched(field, coords, face_sum, basis, geo_grad, test_grad, lift, speeds):
    high = lax.Precision.HIGHEST
    nq, ns = basis.shape
    na = test_grad.shape[0]
    nv = speeds.shape[1]
    nft = lift.shape[1]
    count = field.shape[1]
    values = jnp.einsum("qs,vse->vqe", basis, field.reshape(nv, ns, count), precision=high)
    jac = jnp.einsum("kqs,cse->ckqe", geo_grad, coords.reshape(3, ns, count), precision=high)
    rows = []
    for c in range(3):
        cols = []
        for k in range(3):
            cols.append(
                jac[(c + 1) % 3, (k + 1) % 3] * jac[(c + 2) % 3, (k + 2) % 3]
                - jac[(c + 1) % 3, (k + 2) % 3] * jac[(c + 2) % 3, (k + 1) % 3]
            )
        rows.append(jnp.stack(cols, 0))
    cof = jnp.stack(rows, 0)
    flux = values * (1.0 + 0.5 * jnp.tanh(values))
    weight = jnp.einsum("ckqe,cv->kvqe", cof, speeds, precision=high)
    fhat = weight * flux[None]
    out = jnp.einsum("ikq,kvqe->vie", test_grad.reshape(na, 3, nq), fhat, precision=high)
    out = out + jnp.einsum("if,vfe->vie", lift, face_sum.reshape(nv, nft, count), precision=high)
    return out.reshape(nv * na, count)


def per_device(
    state,
    adjoint,
    geometry,
    face_blocks,
    face_elem,
    move_ids,
    move_counts,
    basis,
    geo_grad,
    test_grad,
    lift,
    speeds,
):
    elems = state.shape[1]
    live, keep = departures(move_ids, move_counts, elems)
    first, second = face_numbers(face_elem, elems)
    flat_ids = move_ids.reshape(-1)
    moving = flat_ids.shape[0]
    face_rows = face_blocks.shape[0]
    moved_faces = jnp.take(
        face_blocks, jnp.concatenate([first[flat_ids], second[flat_ids]]), axis=1
    )
    widths = [state.shape[0], adjoint.shape[0], geometry.shape[0], face_rows, face_rows]
    fields = [
        jnp.take(state, flat_ids, axis=1),
        jnp.take(adjoint, flat_ids, axis=1),
        jnp.take(geometry, flat_ids, axis=1),
        moved_faces[:, :moving],
        moved_faces[:, moving:],
    ]
    record = jnp.concatenate(fields, 0)
    sent = record.reshape(record.shape[0], move_ids.shape[0], move_ids.shape[1]) * live[None]
    rows_ext = with_halo(sent[:, 0:2], (("gx", 1),), 1)
    cols_ext = with_halo(sent[:, 2:4], (("gy", 1),), 1)
    arrived = jnp.concatenate([rows_ext[:, 0], rows_ext[:, 3], cols_ext[:, 0], cols_ext[:, 3]], 1)
    pieces = []
    offset = 0
    for width in widths:
        pieces.append(arrived[offset : offset + width])
        offset = offset + width
    state_out = jnp.concatenate([state * keep, pieces[0]], 1)
    adjoint_out = jnp.concatenate([adjoint * keep, pieces[1]], 1)
    geometry_out = jnp.concatenate([geometry * keep, pieces[2]], 1)
    faces_out = jnp.concatenate([face_blocks * keep[face_elem], pieces[3], pieces[4]], 1)
    residual = enriched(
        pieces[0], pieces[2], pieces[3] + pieces[4], basis, geo_grad, test_grad, lift, speeds
    )
    return (state_out, adjoint_out, geometry_out, faces_out, residual)


def solution(mesh):
    return jax.shard_map(
        per_device,
        mesh=mesh,
        in_specs=(
            P(None, ("gx", "gy")),
            P(None, ("gx", "gy")),
            P(None, ("gx", "gy")),
            P(None, ("gx", "gy")),
            P(("gx", "gy")),
            P(("gx", "gy"), None),
            P(("gx", "gy")),
            P(),
            P(),
            P(),
            P(),
            P(),
        ),
        out_specs=(
            P(None, ("gx", "gy")),
            P(None, ("gx", "gy")),
            P(None, ("gx", "gy")),
            P(None, ("gx", "gy")),
            P(None, ("gx", "gy")),
        ),
        check_vma=False,
    )
```

profile of v0, /device:TPU:29, one launch (start us, length us, event | category | flops | bytes accessed | tf_op | source)
XLA Modules:
  0.0 484.6 jit_solution(120275167382895107)
XLA Ops:
  2.7 5.0 %copy.30 = f32[175,4096]{0,1:T(8,128)} copy(f32[175,4096]{1,0:T(8,128)} %param.13) | data formatting | bytes 5734400 | tf_op args[1]
  7.6 14.2 %gather_fusion = f32[4096,100]{1,0:T(8,128)} fusion(f32[100,4096]{0,1:T(8,128)S(1)} %copy.29, s32[4096]{0:T(1024)S(1)} %broadcast_clamp_fusion.2), kind=kCustom, calls=%fused_computation | custom fusion | bytes 3293184 | tf_op jit(solution)/shard_map/jit(_take)/gather | solution.py:87
  21.8 18.5 %gather_fusion.1 = f32[4096,175]{1,0:T(8,128)} fusion(f32[175,4096]{0,1:T(8,128)} %copy.30, s32[4096]{0:T(1024)S(1)} %broadcast_clamp_fusion.2), kind=kCustom, calls=%fused_computation.1 | custom fusion | bytes 5750784 | tf_op jit(solution)/shard_map/jit(_take)/gather | solution.py:88
  47.6 14.2 %gather_fusion.2 = f32[4096,60]{1,0:T(8,128)} fusion(f32[60,4096]{0,1:T(8,128)S(1)} %copy.31, s32[4096]{0:T(1024)S(1)} %broadcast_clamp_fusion.2), kind=kCustom, calls=%fused_computation.2 | custom fusion | bytes 1982464 | tf_op jit(solution)/shard_map/jit(_take)/gather | solution.py:89
  61.8 4.8 %select_bitcast_fusion.2 = f32[60,4096]{0,1:T(8,128)} fusion(f32[4096,60]{1,0:T(8,128)} %gather_fusion.2, pred[4096]{0:T(1024)(128)(4,1)S(1)} %compare_and_fusion.1), kind=kLoop, calls=%fused_computation.33 | loop fusion | flops 245760 | bytes 1970176 | tf_op jit(solution)/shard_map/jit(_take)/select_n | solution.py:89
  70.0 44.2 %scatter_custom_fusion.2 = s32[4096]{0:T(1024)S(1)} fusion(s32[8192]{0:T(1024)S(1)} %get-tuple-element.23, s32[8192]{0:T(1024)S(1)} %iota.15, s32[]{:T(128)} %constant.38.clone.1), kind=kCustom, calls=%fused_computation.76 | custom fusion | flops 8192 | bytes 16388 | tf_op jit(solution)/shard_map/scatter-max | solution.py:31
  114.2 23.0 %gather_fusion.4 = s32[4096]{0:T(1024)S(1)} fusion(s32[4096]{0:T(1024)S(1)} %scatter_custom_fusion.2, s32[4096]{0:T(1024)S(1)} %broadcast_clamp_fusion.2), kind=kCustom, calls=%fused_computation.4 | custom fusion | bytes 49152 | tf_op jit(solution)/shard_map/gather | solution.py:83
  137.3 44.4 %scatter_custom_fusion.1 = s32[4096]{0:T(1024)S(1)} fusion(s32[8192]{0:T(1024)S(1)} %get-tuple-element.23, s32[8192]{0:T(1024)S(1)} %iota.14, s32[]{:T(128)} %constant.48.clone.1), kind=kCustom, calls=%fused_computation.74 | custom fusion | flops 8192 | bytes 16388 | tf_op jit(solution)/shard_map/scatter-min | solution.py:30
  181.7 23.0 %gather_fusion.3 = s32[4096]{0:T(1024)S(1)} fusion(s32[4096]{0:T(1024)S(1)} %scatter_custom_fusion.1, s32[4096]{0:T(1024)S(1)} %broadcast_clamp_fusion.2), kind=kCustom, calls=%fused_computation.3 | custom fusion | bytes 49152 | tf_op jit(solution)/shard_map/gather | solution.py:83
  204.8 30.0 %gather_fusion.5 = f32[8192,75]{1,0:T(8,128)} fusion(f32[75,8192]{0,1:T(8,128)} %copy.32, s32[8192]{0:T(1024)S(1)} %broadcast_clamp_fusion.1), kind=kCustom, calls=%fused_computation.5 | custom fusion | bytes 4947968 | tf_op jit(solution)/shard_map/jit(_take)/gather | solution.py:82
  234.9 6.2 %select_bitcast_fusion = f32[75,8192]{0,1:T(8,128)S(1)} fusion(f32[8192,75]{1,0:T(8,128)} %gather_fusion.5, pred[8192]{0:T(1024)(128)(4,1)S(1)} %compare_and_fusion), kind=kLoop, calls=%fused_computation.24 | loop fusion | flops 614400 | bytes 4923392 | tf_op jit(solution)/shard_map/jit(_take)/select_n | solution.py:82
  243.5 12.6 %concatenate.52 = f32[485,4096]{0,1:T(8,128)} concatenate(f32[100,4096]{0,1:T(8,128)S(1)} %copy-done.7, f32[175,4096]{0,1:T(8,128)} %select_bitcast_fusion.1, f32[60,4096]{0,1:T(8,128)} %select_bitcast_fusion.2, f32[75,4096]{0,1:T(8,128)} %get-tuple-element.21, f32[75,4096]{0,1:T(8,128)} %get-tuple-element.20), dimensions={0} | concatenate | bytes 15892480 | tf_op jit(solution)/shard_map/concatenate | solution.py:93
  256.1 9.9 %copy.33 = f32[485,4,1024]{2,1,0:T(4,128)} copy(f32[485,4,1024]{0,2,1:T(8,128)} %bitcast.100) | data formatting | bytes 15892480 | tf_op jit(solution)/shard_map/reshape | solution.py:94
  266.1 5.2 %broadcast_multiply_fusion = f32[485,4,1024]{2,1,0:T(4,128)S(1)} fusion(f32[485,4,1024]{2,1,0:T(4,128)} %copy.33, f32[4,1024]{1,0:T(4,128)S(1)} %get-tuple-element.25), kind=kLoop, calls=%fused_computation.26 | loop fusion | flops 1986560 | bytes 15908864 | tf_op jit(solution)/shard_map/mul | solution.py:94
  271.3 7.4 %fusion.26 = (f32[485,1,1024]{2,1,0:T(1,128)}, f32[485,1,1024]{2,1,0:T(1,128)}, f32[485,1,1024]{2,1,0:T(1,128)}, f32[485,1,1024]{2,1,0:T(1,128)}) fusion(f32[485,4,1024]{2,1,0:T(4,128)S(1)} %broadcast_multiply_fusion), kind=kLoop, calls=%fused_computation.86 | loop fusion | bytes 15892480 | tf_op jit(solution)/shard_map/slice | solution.py:12
  281.3 5.0 %collective-permute-start.2 = (f32[485,1,1024]{2,1,0:T(1,128)}, f32[485,1,1024]{2,1,0:T(1,128)}, u32[]{:S(2)}, u32[]{:S(2)}) collective-permute-start(f32[485,1,1024]{2,1,0:T(1,128)} %get-tuple-element.10), channel_id=1, source_target_pairs={{0,1},{1,2},{2,3},{3,4},{4,5},{5,6},{6,7},{7,8},{8,9},{9,10},{10,1... | collective-permute-start | bytes 5959688 | tf_op jit(solution)/shard_map/ppermute | solution.py:14
  293.0 21.9 %scatter_custom_fusion = f32[4096]{0:T(1024)S(1)} fusion(s32[4096]{0:T(1024)S(1)} %bitcast.119, f32[4096]{0:T(1024)S(1)} %bitcast.121, f32[]{:T(128)} %constant.37.clone.1), kind=kCustom, calls=%fused_computation.78 | custom fusion | flops 4096 | bytes 16388 | tf_op jit(solution)/shard_map/scatter-max | solution.py:23
  320.8 45.5 %gather_fusion.6 = f32[8192]{0:T(1024)S(1)} fusion(f32[4096]{0:T(1024)S(1)} %broadcast_subtract_fusion, s32[8192]{0:T(1024)S(1)} %get-tuple-element.22), kind=kCustom, calls=%fused_computation.6 | custom fusion | bytes 98304 | tf_op jit(solution)/shard_map/gather | solution.py:106
  384.3 6.4 %convolution_bitcast_fusion = f32[3,3,46,4096]{3,2,1,0:T(8,128)S(1)} fusion(f32[3,20,4096,1]{2,1,0,3:T(8,128)S(1)} %reshape.640, f32[3,46,20]{1,2,0:T(8,128)S(1)} %copy-done), kind=kOutput, calls=%fused_computation.17 | convolution fusion | flops 406978560 | bytes 7777056 | tf_op jit(solution)/shard_map/kqs,cse->ckqe/dot_general | solution.py:43
  402.5 4.0 add_multiply_fusion
  406.5 5.1 %copy.35 = f32[5,46,4096]{2,0,1:T(8,128)} copy(f32[5,46,4096]{2,1,0:T(8,128)S(1)} %add_multiply_fusion) | data formatting | bytes 7536640 | tf_op jit(solution)/shard_map/mul | solution.py:54
  421.0 31.6 %bitcast_multiply_fusion = f32[3,5,46,4096]{3,1,2,0:T(8,128)S(1)} fusion(f32[5,46,4096]{2,0,1:T(8,128)S(1)} %bitcast.99, f32[3,3,46,4096]{3,2,1,0:T(8,128)} %pad_maximum_fusion.1, f32[3,5]{1,0:T(4,128)S(1)} %copy-done.31), kind=kOutput, calls=%fused_computation.10 | convolution fusion | flops 104570880 | bytes 21856316 | tf_op jit(solution)/shard_map/ckqe,cv->kvqe/dot_general | solution.py:55
  452.6 17.7 %fusion.7 = f32[5,4096,35]{1,2,0:T(8,128)S(1)} fusion(f32[3,5,46,4096]{3,1,2,0:T(8,128)S(1)} %bitcast_multiply_fusion, f32[35,3,46]{2,1,0:T(4,128)S(1)} %reshape.553), kind=kOutput, calls=%fused_computation.23 | convolution fusion | flops 1187020800 | bytes 14191480 | tf_op jit(solution)/shard_map/ikq,kvqe->vie/dot_general | solution.py:57
  475.5 6.0 %pad_maximum_fusion.2 = f32[175,8192]{1,0:T(8,128)} fusion(f32[175,4096]{1,0:T(8,128)} %slice.134, f32[175,4096]{1,0:T(8,128)} %broadcast_multiply_fusion.1), kind=kLoop, calls=%fused_computation.18 | loop fusion | flops 1433600 | bytes 11468800 | tf_op jit(solution)/shard_map/concatenate | solution.py:104
  (127 shorter events, 77.0 us)
Async XLA Ops:
  0.6 383.6 %copy-start = (f32[3,46,20]{1,2,0:T(8,128)S(1)}, f32[3,46,20]{1,2,0:T(8,128)}, u32[]{:S(2)}) copy-start(f32[3,46,20]{1,2,0:T(8,128)} %param.20) | copy-start | bytes 33124
  21.8 18.5 %copy-start.9 = (f32[4096,100]{1,0:T(8,128)S(1)}, f32[4096,100]{1,0:T(8,128)}, u32[]{:S(2)}) copy-start(f32[4096,100]{1,0:T(8,128)} %gather_fusion) | copy-start | bytes 4915204
  40.3 3.1 copy-start.1
  43.4 3.6 copy-start.15
  61.8 4.9 %copy-start.4 = (f32[75,8192]{1,0:T(8,128)S(1)}, f32[75,8192]{1,0:T(8,128)}, u32[]{:S(2)}) copy-start(f32[75,8192]{1,0:T(8,128)} %param.15) | copy-start | bytes 7372804
  66.7 3.3 copy-start.28
  256.1 9.9 %copy-start.32 = (s32[4]{0:T(128)S(1)}, s32[4]{0:T(128)}, u32[]{:S(2)}) copy-start(s32[4]{0:T(128)} %param.18) | copy-start | bytes 52
  278.7 39.0 %copy-start.2 = (f32[175,4096]{1,0:T(8,128)S(1)}, f32[175,4096]{1,0:T(8,128)}, u32[]{:S(2)}) copy-start(f32[175,4096]{1,0:T(8,128)} %param.13) | copy-start | bytes 8601604
  278.7 89.4 %collective-permute-start.3 = (f32[485,1,1024]{2,1,0:T(1,128)}, f32[485,1,1024]{2,1,0:T(1,128)}, u32[]{:S(2)}, u32[]{:S(2)}) collective-permute-start(f32[485,1,1024]{2,1,0:T(1,128)} %get-tuple-element.9), channel_id=1, source_target_pairs={{1,0},{2,1},{3,2},{4,3},{5,4},{6,5},{7,6},{8,7},{9,8},{10,9},{11,1... | collective-permute-start | bytes 5959688 | tf_op jit(solution)/shard_map/ppermute | solution.py:15
  281.3 88.8 %collective-permute-start.2 = (f32[485,1,1024]{2,1,0:T(1,128)}, f32[485,1,1024]{2,1,0:T(1,128)}, u32[]{:S(2)}, u32[]{:S(2)}) collective-permute-start(f32[485,1,1024]{2,1,0:T(1,128)} %get-tuple-element.10), channel_id=1, source_target_pairs={{0,1},{1,2},{2,3},{3,4},{4,5},{5,6},{6,7},{7,8},{8,9},{9,10},{10,1... | collective-permute-start | bytes 5959688 | tf_op jit(solution)/shard_map/ppermute | solution.py:14
  286.4 85.8 %collective-permute-start.1 = (f32[485,1,1024]{2,1,0:T(1,128)}, f32[485,1,1024]{2,1,0:T(1,128)}, u32[]{:S(2)}, u32[]{:S(2)}) collective-permute-start(f32[485,1,1024]{2,1,0:T(1,128)} %get-tuple-element.11), channel_id=1, source_target_pairs={{16,0},{32,16},{48,32},{64,48},{80,64},{96,80},{112,96},{17,1},{33... | collective-permute-start | bytes 5959688 | tf_op jit(solution)/shard_map/ppermute | solution.py:15
  289.5 84.6 %collective-permute-start = (f32[485,1,1024]{2,1,0:T(1,128)}, f32[485,1,1024]{2,1,0:T(1,128)}, u32[]{:S(2)}, u32[]{:S(2)}) collective-permute-start(f32[485,1,1024]{2,1,0:T(1,128)} %get-tuple-element.8), channel_id=1, source_target_pairs={{0,16},{16,32},{32,48},{48,64},{64,80},{80,96},{96,112},{1,17},{17... | collective-permute-start | bytes 5959688 | tf_op jit(solution)/shard_map/ppermute | solution.py:14
  320.8 45.5 %copy-start.27 = (f32[35,138]{1,0:T(8,128)S(1)}, f32[35,138]{1,0:T(8,128)}, u32[]{:S(2)}) copy-start(f32[35,138]{1,0:T(8,128)} %param.21) | copy-start | bytes 57964
  320.8 45.6 %copy-start.5 = (f32[75,8192]{1,0:T(8,128)S(1)}, f32[75,8192]{1,0:T(8,128)}, u32[]{:S(2)}) copy-start(f32[75,8192]{1,0:T(8,128)} %param.15) | copy-start | bytes 7372804
  406.5 5.1 %copy-start.13 = (f32[75,4096]{1,0:T(8,128)S(1)}, f32[75,4096]{1,0:T(8,128)}, u32[]{:S(2)}) copy-start(f32[75,4096]{1,0:T(8,128)} %get-tuple-element.5) | copy-start | bytes 3686404
  413.5 2.5 copy-start.23
  416.0 4.3 slice-start
  416.4 4.5 slice-start.1
  416.4 4.5 copy-start.31
  452.6 17.7 %copy-start.14 = (f32[5,15,4096]{2,1,0:T(8,128)S(1)}, f32[5,15,4096]{2,1,0:T(8,128)}, u32[]{:S(2)}) copy-start(f32[5,15,4096]{2,1,0:T(8,128)} %reshape.554) | copy-start | bytes 3686404
  452.6 17.7 %copy-start.30 = (f32[35,15]{0,1:T(8,128)S(1)}, f32[35,15]{0,1:T(8,128)}, u32[]{:S(2)}) copy-start(f32[35,15]{0,1:T(8,128)} %param.22) | copy-start | bytes 6304
  475.5 6.0 %copy-start.3 = (f32[75,8192]{1,0:T(8,128)S(1)}, f32[75,8192]{1,0:T(8,128)}, u32[]{:S(2)}) copy-start(f32[75,8192]{1,0:T(8,128)} %broadcast_multiply_fusion.2) | copy-start | bytes 7372804
  475.5 6.0 %copy-start.11 = (f32[75,4096]{1,0:T(8,128)S(1)}, f32[75,4096]{1,0:T(8,128)}, u32[]{:S(2)}) copy-start(f32[75,4096]{1,0:T(8,128)} %get-tuple-element.6) | copy-start | bytes 3686404
  475.5 6.0 %copy-start.12 = (f32[75,4096]{1,0:T(8,128)S(1)}, f32[75,4096]{1,0:T(8,128)}, u32[]{:S(2)}) copy-start(f32[75,4096]{1,0:T(8,128)} %get-tuple-element.7) | copy-start | bytes 3686404
  (15 other events, 30.0 us)
where the time goes:
time: 491 us; the launch traced here: 485 us
  local copies, waits for them, and re-layouts  237 us (48%)
  other arithmetic  169 us (34%)
  matrix products  62.9 us (13%)
  starting transfers between devices  14.3 us (3%)
    gather x1, local copies, waits for them, and re-layouts, per_device(): keep[face_elem]  45.5 us
    another operation x1, other arithmetic, face_numbers(): first = jnp.full((elems,), nfaces, jnp.int32).at[owners].min(where)  44.4 us
    another operation x1, other arithmetic, face_numbers(): second = jnp.zeros((elems,), jnp.int32).at[owners].max(where)  44.2 us
    dot_general x1, matrix products, enriched(): weight = jnp.einsum('ckqe,cv->kvqe', cof, speeds, precision=high)  31.6 us
    gather x1, local copies, waits for them, and re-layouts, per_device(): jnp.take(face_blocks, jnp.concatenate([first[flat_ids], second[flat_ids]]...  30 us
    unnamed x81, local copies, waits for them, and re-layouts  23.2 us
    gather x1, local copies, waits for them, and re-layouts, per_device(): second[flat_ids]  23 us
    gather x1, local copies, waits for them, and re-layouts, per_device(): first[flat_ids]  23 us
  transfers between devices with their start and end apart: 4, of which 0 were waited for; matrix products, arithmetic and copies ran while one was open for 17% of the time, Pallas kernels for 0%

commit v1 on v0

v1 whole, which is shorter than its diff:
```python
import functools

import jax
import jax.numpy as jnp
from jax import lax
from jax.experimental import pallas as pl
from jax.experimental.pallas import tpu as pltpu
from jax.sharding import PartitionSpec as P

F32 = jnp.float32
BF16 = jnp.bfloat16
I32 = jnp.int32
VMEM = pltpu.VMEM
L = 128
NV, NS, NA, NQ, NFT = 5, 20, 35, 46, 15
QP = 48
E = 4096
CAP = 1024
RS, RA, RG, RF = NV * NS, NV * NA, 3 * NS, NV * NFT
RSG = RS + RG
VALS = NV * QP
WROWS = VALS + 9 * QP


def spec(space=pltpu.VMEM):
    return pl.BlockSpec(memory_space=space)


ANY = pl.ANY
SMEM = pltpu.SMEM


def params(mib):
    return pltpu.CompilerParams(vmem_limit_bytes=mib << 20)


COST = pl.CostEstimate(flops=1, transcendentals=0, bytes_accessed=1)


def padded(block, rows):
    return jnp.concatenate([block, jnp.zeros((rows - block.shape[0], L), F32)], 0)


def at(c):
    return pl.ds(pl.multiple_of(c * L, L), L)


def copy_rows(ids, row, pairs):
    for j in range(L):
        e = ids[row, j]
        for src, dst in pairs:
            dst[pl.ds(j, 1), :] = src[pl.ds(e, 1), :]


def ids_to_scalar(ids_v, ids, sems, sides):
    copies = []
    for side in sides:
        for b in range(CAP // L):
            r = side * (CAP // L) + b
            copies.append(
                pltpu.make_async_copy(
                    ids_v.at[pl.ds(side, 1), pl.ds(b * L, L)], ids.at[pl.ds(r, 1), :], sems.at[r]
                )
            )
    for c in copies:
        c.start()
    return copies


def live_lanes(cnt, side, block):
    return lax.broadcasted_iota(I32, (1, L), 1) + block * L < cnt[side]


def ids_scratch():
    return [pltpu.SMEM((E // L, L), I32), pltpu.SemaphoreType.DMA((E // L,))]


def pack_loop(ids, cnt, sides, srcs, bufs, emit):
    for s, side in enumerate(sides):

        def two(i, carry, s=s, side=side):
            for h in range(2):
                block = i * 2 + h
                copy_rows(ids, side * (CAP // L) + block, list(zip(srcs, bufs[h])))
                live = live_lanes(cnt, side, block)
                emit(s, block, live, [b[...].T for b in bufs[h]])
            return carry

        lax.fori_loop(0, CAP // L // 2, two, 0)


def sg_first_body(ids_v, cnt, st, ge, up, dn, xs, xg, a0, a1, b0, b1, ids, idsem):
    moved = ids_to_scalar(ids_v, ids, idsem, (2, 3))

    def fwd(c, carry):
        xs[at(c), :] = padded(st[:, at(c)], L).T
        xg[at(c), :] = padded(ge[:, at(c)], L).T
        return carry

    lax.fori_loop(0, E // L, fwd, 0, unroll=2)
    for c in moved:
        c.wait()
    outs = (up, dn)

    def emit(s, block, live, parts):
        outs[s][0:RS, at(block)] = jnp.where(live, parts[0][:RS], 0.0)
        outs[s][RS:RSG, at(block)] = jnp.where(live, parts[1][:RG], 0.0)

    pack_loop(ids, cnt, (3, 2), (xs, xg), ((a0, a1), (b0, b1)), emit)


def sg_first(ids, cnt, st, ge):
    return pl.pallas_call(
        sg_first_body,
        out_shape=[jax.ShapeDtypeStruct((RSG, CAP), F32)] * 2,
        in_specs=[spec(), spec(SMEM), spec(), spec()],
        out_specs=[spec(), spec()],
        scratch_shapes=[VMEM((E, L), F32)] * 2 + [VMEM((L, L), F32)] * 4 + ids_scratch(),
        compiler_params=params(12),
        cost_estimate=COST,
        name="pack_sg_gy",
    )(ids, cnt, st, ge)


def sg_second_body(
    ids_v, cnt, keep, st, ge, up, dn, st_out, ge_out, xs, xg, ks, kg, a0, a1, b0, b1, sems, ids, idsem,
):
    moved = ids_to_scalar(ids_v, ids, idsem, (0, 1))

    def fwd(c, carry):
        k = keep[pl.ds(c, 1), :]
        s, g = st[:, at(c)], ge[:, at(c)]
        ks[:, at(c)] = s * k
        kg[:, at(c)] = g * k
        xs[at(c), :] = padded(s, L).T
        xg[at(c), :] = padded(g, L).T
        return carry

    lax.fori_loop(0, E // L, fwd, 0, unroll=2)
    c0 = pltpu.make_async_copy(ks, st_out.at[:, pl.ds(0, E)], sems.at[0])
    c1 = pltpu.make_async_copy(kg, ge_out.at[:, pl.ds(0, E)], sems.at[1])
    c0.start()
    c1.start()
    for c in moved:
        c.wait()
    outs = (up, dn)

    def emit(s, block, live, parts):
        outs[s][0:RS, at(block)] = jnp.where(live, parts[0][:RS], 0.0)
        outs[s][RS:RSG, at(block)] = jnp.where(live, parts[1][:RG], 0.0)

    pack_loop(ids, cnt, (1, 0), (xs, xg), ((a0, a1), (b0, b1)), emit)
    c0.wait()
    c1.wait()


def sg_second(ids, cnt, keep, st, ge):
    return pl.pallas_call(
        sg_second_body,
        out_shape=[jax.ShapeDtypeStruct((RSG, CAP), F32)] * 2
        + [jax.ShapeDtypeStruct((RS, 2 * E), F32), jax.ShapeDtypeStruct((RG, 2 * E), F32)],
        in_specs=[spec(), spec(SMEM), spec(), spec(), spec()],
        out_specs=[spec(), spec(), spec(ANY), spec(ANY)],
        scratch_shapes=[VMEM((E, L), F32)] * 2
        + [VMEM((RS, E), F32), VMEM((RG, E), F32)]
        + [VMEM((L, L), F32)] * 4
        + [pltpu.SemaphoreType.DMA((2,))]
        + ids_scratch(),
        compiler_params=params(16),
        cost_estimate=COST,
        name="pack_sg_gx",
    )(ids, cnt, keep, st, ge)


def adj_body(
    ids_v, cnt, keep, ad, yu, yd, xu, xd, ad_out, x0, x1, ka, a0, a1, b0, b1, sem, ids, idsem,
):
    moved = ids_to_scalar(ids_v, ids, idsem, range(4))

    def fwd(c, carry):
        k = keep[pl.ds(c, 1), :]
        p, q = ad[0:L, at(c)], ad[L:RA, at(c)]
        ka[0:L, at(c)] = p * k
        ka[L:RA, at(c)] = q * k
        x0[at(c), :] = p.T
        x1[at(c), :] = padded(q, L).T
        return carry

    lax.fori_loop(0, E // L, fwd, 0, unroll=2)
    c0 = pltpu.make_async_copy(ka, ad_out.at[:, pl.ds(0, E)], sem.at[0])
    c0.start()
    for c in moved:
        c.wait()
    outs = (yu, yd, xu, xd)

    def emit(s, block, live, parts):
        outs[s][0:L, at(block)] = jnp.where(live, parts[0], 0.0)
        outs[s][L:RA, at(block)] = jnp.where(live, parts[1][: RA - L], 0.0)

    pack_loop(ids, cnt, (3, 2, 1, 0), (x0, x1), ((a0, a1), (b0, b1)), emit)
    c0.wait()


def adj_pack(ids, cnt, keep, ad):
    return pl.pallas_call(
        adj_body,
        out_shape=[jax.ShapeDtypeStruct((RA, CAP), F32)] * 4
        + [jax.ShapeDtypeStruct((RA, 2 * E), F32)],
        in_specs=[spec(), spec(SMEM), spec(), spec()],
        out_specs=[spec()] * 4 + [spec(ANY)],
        scratch_shapes=[VMEM((E, L), F32)] * 2
        + [VMEM((RA, E), F32)]
        + [VMEM((L, L), F32)] * 4
        + [pltpu.SemaphoreType.DMA((1,))]
        + ids_scratch(),
        compiler_params=params(18),
        cost_estimate=COST,
        name="pack_adj",
    )(ids, cnt, keep, ad)


def dot_nt(a, b):
    return lax.dot_general(a, b, (((1,), (1,)), ((), ())), preferred_element_type=F32)


def dot_nn(a, b):
    return lax.dot_general(a, b, (((1,), (0,)), ((), ())), preferred_element_type=F32)


def faces_body(
    ids_v, owners, cnt, fb, yu, yd, xu, xd, keep, fb_out,
    xf, kf, fkeep, sums, depart, nums, nums_s, a0, a1, b0, b1, sems,
):
    hi32 = lax.broadcasted_iota(I32, (32, L), 0)
    lo128 = lax.broadcasted_iota(I32, (L, L), 0)
    lane = lax.broadcasted_iota(I32, (1, L), 1)
    sq = lane * lane
    weights = [w.astype(F32) for w in (lane, sq >> 7, sq & 127)]
    nf = 2 * E // L
    ne = E // L
    unroll = 4

    def onehots(row):
        mine = hi32 == (row >> 7)
        low = (lo128 == (row & 127)).astype(F32).astype(BF16)
        return mine, low

    sums[...] = jnp.zeros_like(sums)
    depart[...] = jnp.zeros_like(depart)

    def face_sums(g, carry):
        s1, s2 = carry
        for u in range(unroll):
            i = g * unroll + u
            mine, low = onehots(owners[pl.ds(i, 1), :])
            ones = mine.astype(F32)
            left = jnp.concatenate([ones] + [ones * w for w in weights], 0).astype(BF16)
            r = dot_nt(left, low).astype(I32)
            n, l, q = r[0:32], r[32:64], r[64:96] * 128 + r[96:128]
            base = i * L
            s1 = s1 + base * n + l
            s2 = s2 + base * base * n + 2 * base * l + q
        return s1, s2

    zero = jnp.zeros((32, L), I32)
    s1, s2 = lax.fori_loop(0, nf // unroll, face_sums, (zero, zero))
    gap = jnp.floor(jnp.sqrt((2 * s2 - s1 * s1).astype(F32)) + 0.5).astype(I32)
    first, second = (s1 - gap) >> 1, (s1 + gap) >> 1
    table = jnp.concatenate([first >> 7, first & 127, second >> 7, second & 127], 0)
    table = table.astype(F32).astype(BF16)

    def slots(g, dep, side):
        for u in range(unroll):
            b = g * unroll + u
            r = side * (CAP // L) + b
            mine, low = onehots(ids_v[pl.ds(side, 1), at(b)])
            live = (lane + b * L < cnt[side]).astype(F32)
            ones = mine.astype(F32)
            dep = dep + dot_nt((ones * live).astype(BF16), low)
            found = dot_nn(table, low)
            pick = [
                jnp.sum(jnp.where(mine, found[32 * m : 32 * m + 32], 0.0), 0, keepdims=True)
                for m in range(4)
            ]
            nums[pl.ds(r, 1), :] = (pick[0] * 128.0 + pick[1]).astype(I32)
            nums[pl.ds(ne + r, 1), :] = (pick[2] * 128.0 + pick[3]).astype(I32)
        return dep

    dep = jnp.zeros((32, L), F32)
    for side in range(4):
        dep = lax.fori_loop(0, CAP // L // unroll, functools.partial(slots, side=side), dep)
    to_scalar = pltpu.make_async_copy(nums, nums_s, sems.at[1])
    to_scalar.start()
    kept = 1.0 - jnp.minimum(dep, 1.0)
    keep[...] = kept
    kept16 = kept.astype(BF16)

    def fwd(g, carry):
        for u in range(2):
            c = g * 2 + u
            mine, low = onehots(owners[pl.ds(c, 1), :])
            k = jnp.sum(jnp.where(mine, dot_nn(kept16, low), 0.0), 0, keepdims=True)
            f = fb[:, at(c)]
            kf[:, at(c)] = f * k
            xf[at(c), :] = padded(f, L).T
        return carry

    lax.fori_loop(0, nf // 2, fwd, 0)
    c0 = pltpu.make_async_copy(kf, fb_out.at[:, pl.ds(0, 2 * E)], sems.at[0])
    c0.start()
    to_scalar.wait()
    outs = (yu, yd, xu, xd)
    bufs = ((a0, a1), (b0, b1))
    for s, side in enumerate((3, 2, 1, 0)):

        def two(i, carry, s=s, side=side):
            for h in range(2):
                block = i * 2 + h
                row = side * (CAP // L) + block
                copy_rows(nums_s, row, [(xf, bufs[h][0])])
                copy_rows(nums_s, ne + row, [(xf, bufs[h][1])])
                live = live_lanes(cnt, side, block)
                outs[s][0:RF, at(block)] = jnp.where(live, bufs[h][0][...].T[:RF], 0.0)
                outs[s][RF : 2 * RF, at(block)] = jnp.where(live, bufs[h][1][...].T[:RF], 0.0)
            return carry

        lax.fori_loop(0, CAP // L // 2, two, 0)
    c0.wait()


def faces_pack(ids, owners, cnt, fb):
    return pl.pallas_call(
        faces_body,
        out_shape=[jax.ShapeDtypeStruct((2 * RF, CAP), F32)] * 4
        + [jax.ShapeDtypeStruct((32, L), F32), jax.ShapeDtypeStruct((RF, 4 * E), F32)],
        in_specs=[spec(), spec(), spec(SMEM), spec()],
        out_specs=[spec()] * 5 + [spec(ANY)],
        scratch_shapes=[
            VMEM((2 * E, L), F32),
            VMEM((RF, 2 * E), F32),
            VMEM((64, L), F32),
            VMEM((8, L), F32),
            VMEM((8, L), F32),
            VMEM((64, L), I32),
            SMEM((64, L), I32),
        ]
        + [VMEM((L, L), F32)] * 4
        + [pltpu.SemaphoreType.DMA((2,))],
        compiler_params=params(17),
        cost_estimate=COST,
        name="pack_faces",
    )(ids, owners, cnt, fb)


NB = 256


def split(x):
    hi = x.astype(BF16)
    return hi, (x - hi.astype(F32)).astype(BF16)


def arrive_body(
    part, first_call, speeds, basis, grad, test, lift, sg_a, sg_b, fp_a, fp_b, *rest,
):
    if first_call:
        st_in, ge_in, fb_in, st_out, ge_out, fb_out, res_out = rest[:7]
        rest = rest[7:]
    else:
        st_in, ge_in, fb_in, res_in, st_out, ge_out, fb_out, res_out = rest[:8]
        rest = rest[8:]
    wf, w3, tt, lf, ll, vj, fh, ks, kg, k1, k2, kr, sems = rest
    cols = pl.ds(E + part * 2 * CAP, 2 * CAP)

    wf[...] = jnp.zeros_like(wf)
    for v in range(NV):
        wf[v * NS : (v + 1) * NS, v * QP : v * QP + NQ] = basis[...]
    for c in range(3):
        for k in range(3):
            r = VALS + (c * 3 + k) * QP
            wf[RS + c * NS : RS + (c + 1) * NS, r : r + NQ] = grad[k]
    for r in range(0, 768, L):
        top = wf[0:L, r : r + L].T
        low = wf[L : 2 * L, r : r + L].T
        wide = jnp.concatenate([top, low], 1)[: min(L, WROWS - r)]
        wh, wl = split(wide[:, 0:RSG])
        here = slice(r, min(r + L, WROWS))
        w3[here, 0:RSG] = wh
        w3[here, RSG : 2 * RSG] = wh
        w3[here, 2 * RSG : 3 * RSG] = wl
    lf[...] = jnp.zeros_like(lf)
    lf[0:NA, 0 : 3 * QP] = jnp.zeros((NA, 3 * QP), F32)
    for k in range(3):
        lf[0:NA, k * QP : k * QP + NQ] = test[:, k * NQ : (k + 1) * NQ]
    th, tl = split(lf[0:48, 0 : 3 * QP])
    tt[0:48, :] = th
    tt[48:96, :] = tl
    lf[...] = jnp.zeros_like(lf)
    for v in range(NV):
        lf[v * NFT : (v + 1) * NFT, v * 40 : v * 40 + NA] = lift[...]
    lt = jnp.concatenate([lf[0:L, 0:L].T, lf[0:L, L : 2 * L].T], 0)
    lh, l2 = split(lt[0:208, 0:80])
    ll[0:208, :] = lh
    ll[208:416, :] = l2

    def block(b, carry, sg, fp, d):
        src = pl.ds(pl.multiple_of(b * NB, NB), NB)
        dst = pl.ds(pl.multiple_of(d * CAP + b * NB, NB), NB)
        x = sg[:, src]
        ks[:, dst] = x[0:RS]
        kg[:, dst] = x[RS:RSG]
        f1, f2 = fp[0:RF, src], fp[RF : 2 * RF, src]
        k1[:, dst] = f1
        k2[:, dst] = f2
        hi, lo = split(x)
        vj[...] = dot_nn(w3[...], jnp.concatenate([hi, lo, hi], 0))
        for t in range(QP // 16):
            for h in range(NB // L):
                lanes = slice(h * L, (h + 1) * L)

                def part_of(r):
                    return vj[r + 16 * t : r + 16 * t + 16, lanes]

                jac = [[part_of(VALS + (c * 3 + k) * QP) for k in range(3)] for c in range(3)]
                flux = []
                for v in range(NV):
                    u = part_of(v * QP)
                    flux.append(u + u * (0.5 * jnp.tanh(u)))
                for k in range(3):
                    k1_, k2_ = (k + 1) % 3, (k + 2) % 3
                    cof = []
                    for c in range(3):
                        c1, c2 = (c + 1) % 3, (c + 2) % 3
                        cof.append(jac[c1][k1_] * jac[c2][k2_] - jac[c1][k2_] * jac[c2][k1_])
                    for v in range(NV):
                        w = cof[0] * speeds[0, v] + cof[1] * speeds[1, v] + cof[2] * speeds[2, v]
                        fhi, flo = split(w * flux[v])
                        r = k * QP + 16 * t
                        fh[v, 0, r : r + 16, lanes] = fhi
                        fh[v, 1, r : r + 16, lanes] = flo
        fs = jnp.concatenate([f1 + f2, jnp.zeros((80 - RF, NB), F32)], 0)
        shi, slo = split(fs)
        m1 = dot_nn(ll[...], shi)
        lifted = m1[0:208] + m1[208:416] + dot_nn(ll[0:208, :], slo)
        for v in range(NV):
            d1 = dot_nn(tt[...], fh[v, 0])
            d2 = dot_nn(tt[0:48, :], fh[v, 1])
            total = d1[0:40] + d1[48:88] + d2[0:40] + lifted[40 * v : 40 * v + 40]
            kr[NA * v : NA * (v + 1), dst] = total[0:NA]
        return carry

    for d, (sg, fp) in enumerate(((sg_a, fp_a), (sg_b, fp_b))):
        lax.fori_loop(0, CAP // NB, functools.partial(block, sg=sg, fp=fp, d=d), 0)
    copies = (
        (ks, st_out.at[:, cols]),
        (kg, ge_out.at[:, cols]),
        (k1, fb_out.at[:, pl.ds(2 * E + part * 2 * CAP, 2 * CAP)]),
        (k2, fb_out.at[:, pl.ds(3 * E + part * 2 * CAP, 2 * CAP)]),
        (kr, res_out.at[:, pl.ds(part * 2 * CAP, 2 * CAP)]),
    )
    copies = [pltpu.make_async_copy(s, t, sems.at[m]) for m, (s, t) in enumerate(copies)]
    for c in copies:
        c.start()
    for c in copies:
        c.wait()


def arrive(part, weights, pieces, outs):
    speeds, basis, grad, test, lift = weights
    first_call = len(outs) == 3
    shapes = [
        jax.ShapeDtypeStruct((RS, 2 * E), F32),
        jax.ShapeDtypeStruct((RG, 2 * E), F32),
        jax.ShapeDtypeStruct((RF, 4 * E), F32),
        jax.ShapeDtypeStruct((RA, E), F32),
    ]
    return pl.pallas_call(
        functools.partial(arrive_body, part, first_call),
        out_shape=shapes,
        in_specs=[spec(SMEM)] + [spec()] * 8 + [spec(ANY)] * len(outs),
        out_specs=[spec(ANY)] * 4,
        input_output_aliases={9 + i: i for i in range(len(outs))},
        scratch_shapes=[
            VMEM((256, 768), F32),
            VMEM((WROWS, 3 * RSG), BF16),
            VMEM((96, 3 * QP), BF16),
            VMEM((208, 256), F32),
            VMEM((416, 80), BF16),
            VMEM((WROWS, NB), F32),
            VMEM((NV, 2, 3 * QP, NB), BF16),
            VMEM((RS, 2 * CAP), F32),
            VMEM((RG, 2 * CAP), F32),
            VMEM((RF, 2 * CAP), F32),
            VMEM((RF, 2 * CAP), F32),
            VMEM((RA, 2 * CAP), F32),
            pltpu.SemaphoreType.DMA((5,)),
        ],
        compiler_params=params(14),
        cost_estimate=COST,
        name="arrive_gy" if part else "arrive_gx",
    )(speeds, basis, grad, test, lift, *pieces, *outs)


def place_body(part, a, b, ad_in, ad_out, sems):
    copies = [
        pltpu.make_async_copy(src, ad_out.at[:, pl.ds(E + (part * 2 + q) * CAP, CAP)], sems.at[q])
        for q, src in enumerate((a, b))
    ]
    for c in copies:
        c.start()
    for c in copies:
        c.wait()


def place(part, pieces, ad_out):
    return pl.pallas_call(
        functools.partial(place_body, part),
        out_shape=jax.ShapeDtypeStruct((RA, 2 * E), F32),
        in_specs=[spec(), spec(), spec(ANY)],
        out_specs=spec(ANY),
        input_output_aliases={2: 0},
        scratch_shapes=[pltpu.SemaphoreType.DMA((2,))],
        compiler_params=params(4),
        cost_estimate=COST,
        name="place_gy" if part else "place_gx",
    )(*pieces, ad_out)


def after(value, done):
    return lax.optimization_barrier((value, done))


def exchange(axis, toward_high, toward_low):
    size = lax.axis_size(axis)
    up = [(i, i + 1) for i in range(size - 1)]
    down = [(j, i) for i, j in up]
    return lax.ppermute(toward_high, axis, up), lax.ppermute(toward_low, axis, down)


def per_device(
    state, adjoint, geometry, face_blocks, face_elem, move_ids, move_counts,
    basis, geo_grad, test_grad, lift, speeds,
):
    ids = move_ids
    owners = face_elem.reshape(2 * E // L, L)
    sgy = sg_first(ids, move_counts, state, geometry)
    sg_y = exchange("gy", *sgy)
    face_blocks, _ = after(face_blocks, sgy)
    fyu, fyd, fxu, fxd, keep, faces_out = faces_pack(ids, owners, move_counts, face_blocks)
    fp_y = exchange("gy", fyu, fyd)
    sxu, sxd, state_out, geometry_out = sg_second(ids, move_counts, keep, state, geometry)
    sg_x = exchange("gx", sxu, sxd)
    fp_x = exchange("gx", fxu, fxd)
    adjoint, _ = after(adjoint, (sxu, sxd))
    ayu, ayd, axu, axd, adjoint_out = adj_pack(ids, move_counts, keep, adjoint)
    ad_y = exchange("gy", ayu, ayd)
    ad_x = exchange("gx", axu, axd)
    weights = (speeds, basis.T, geo_grad.transpose(0, 2, 1), test_grad, lift.T)
    outs = arrive(0, weights, (*sg_x, *fp_x), (state_out, geometry_out, faces_out))
    adjoint_out = place(0, ad_x, adjoint_out)
    state_out, geometry_out, faces_out, residual = arrive(1, weights, (*sg_y, *fp_y), outs)
    adjoint_out = place(1, ad_y, adjoint_out)
    return state_out, adjoint_out, geometry_out, faces_out, residual


def solution(mesh):
    cols = P(None, ("gx", "gy"))
    flat = P(("gx", "gy"))
    return jax.shard_map(
        per_device,
        mesh=mesh,
        in_specs=(cols, cols, cols, cols, flat, P(("gx", "gy"), None), flat, P(), P(), P(), P(), P()),
        out_specs=(cols, cols, cols, cols, cols),
        check_vma=False,
    )
```

time: 491 us -> 133 us (0.27)
  local copies, waits for them, and re-layouts: 237 us -> 8.11 us
  other arithmetic: 169 us -> 0 us
  Pallas kernels: 0 us -> 68.7 us
  matrix products: 62.9 us -> 0 us
  starting transfers between devices: 14.3 us -> 34.2 us
  waiting for transfers between devices: 0.01 us -> 18.3 us
    gather x7 -> x0, local copies, waits for them, and re-layouts: 168 us -> none  [the longest x1 45.5 us: per_device(): keep[face_elem]]
    another operation x6 -> x0, other arithmetic: 116 us -> none  [the longest x1 44.4 us: face_numbers(): first = jnp.full((elems,), nfaces, jnp.int32).at[owners].min(where)]
    pallas_call x0 -> x8, Pallas kernels: none -> 68.7 us  [the longest x2 21.5 us: arrive(): pl.pallas_call(functools.partial(arrive_body, part, first_call), out_shap...]
    dot_general x5 -> x0, matrix products: 62.9 us -> none  [the longest x1 31.6 us: enriched(): weight = jnp.einsum('ckqe,cv->kvqe', cof, speeds, precision=high)]
    ppermute x4 -> x12, starting transfers between devices: 14.3 us -> 34.2 us  [the longest x6 19.6 us: exchange(): lax.ppermute(toward_high, axis, up)]
    ppermute x4 -> x12, waiting for transfers between devices: 0.01 us -> 18.3 us  [the longest x6 18.2 us: exchange(): lax.ppermute(toward_low, axis, down)]
    select_n x6 -> x0, other arithmetic: 17.8 us -> none  [the longest x2 6.26 us: per_device(): jnp.take(face_blocks, jnp.concatenate([first[flat_ids], second[flat_ids]]...]
    reshape x6 -> x0, local copies, waits for them, and re-layouts: 15.9 us -> none  [the longest x1 9.91 us: per_device(): record.reshape(record.shape[0], move_ids.shape[0], move_ids.shape[1])]
  transfers between devices with their start and end apart: 4 -> 12, of which waited for: 0 -> 1; matrix products, arithmetic and copies ran while one was open for 17% -> 0% of each run, Pallas kernels for 0% -> 31%
where the time goes in v1:
time: 133 us; the launch traced here: 130 us
  Pallas kernels  68.7 us (52%)
  starting transfers between devices  34.2 us (26%)
  waiting for transfers between devices  18.3 us (14%)
  local copies, waits for them, and re-layouts  8.11 us (6%)
    pallas_call x2, Pallas kernels, arrive(): pl.pallas_call(functools.partial(arrive_body, part, first_call), out_shap...  21.5 us
    pallas_call x1, Pallas kernels, faces_pack(): pl.pallas_call(faces_body, out_shape=[jax.ShapeDtypeStruct((2 * RF, CAP),...  20.2 us
    ppermute x6, starting transfers between devices, exchange(): lax.ppermute(toward_high, axis, up)  19.6 us
    ppermute x6, waiting for transfers between devices, exchange(): lax.ppermute(toward_low, axis, down)  18.2 us
    ppermute x6, starting transfers between devices, exchange(): lax.ppermute(toward_low, axis, down)  14.5 us
    pallas_call x1, Pallas kernels, adj_pack(): pl.pallas_call(adj_body, out_shape=[jax.ShapeDtypeStruct((RA, CAP), F32)]...  11.2 us
    unnamed x36, local copies, waits for them, and re-layouts  8.11 us
    pallas_call x1, Pallas kernels, sg_second(): pl.pallas_call(sg_second_body, out_shape=[jax.ShapeDtypeStruct((RSG, CAP)...  6.83 us
  transfers between devices with their start and end apart: 12, of which 1 were waited for; matrix products, arithmetic and copies ran while one was open for 0% of the time, Pallas kernels for 31%

profile of v1, /device:TPU:29, one launch (start us, length us, event | category | flops | bytes accessed | tf_op | source)
XLA Modules:
  0.0 130.5 jit_solution(10597557085402285750)
XLA Ops:
  0.6 1.4 %copy-done = f32[100,4096]{1,0:T(8,128)S(1)} copy-done((f32[100,4096]{1,0:T(8,128)S(1)}, f32[100,4096]{1,0:T(8,128)}, u32[]{:S(2)}) %copy-start) | copy-done | bytes 1638424
  2.1 1.2 copy-done.2
  4.7 6.8 %pack_sg_gy.1 = (f32[160,1024]{1,0:T(8,128)S(1)}, f32[160,1024]{1,0:T(8,128)S(1)}) custom-call(s32[4,1024]{1,0:T(4,128)S(1)} %copy-done.6, s32[4]{0:T(128)S(1)} %copy-done.14, f32[100,4096]{1,0:T(8,128)S(1)} %copy-done, f32[60,4096]{1,0:T(8,128)S(1)} %copy-done.2), custom_call_target="tpu_custom_call" | custom-call | flops 1 | bytes 1 | tf_op jit(solution)/shard_map/pack_sg_gy/pallas_call | solution.py:113
  11.5 1.9 %copy-done.5 = f32[75,8192]{1,0:T(8,128)S(1)} copy-done((f32[75,8192]{1,0:T(8,128)S(1)}, f32[75,8192]{1,0:T(8,128)}, u32[]{:S(2)}) %copy-start.5) | copy-done | bytes 2457624
  15.5 20.2 %pack_faces.1 = (f32[150,1024]{1,0:T(8,128)S(1)}, f32[150,1024]{1,0:T(8,128)S(1)}, f32[150,1024]{1,0:T(8,128)S(1)}, f32[150,1024]{1,0:T(8,128)S(1)}, f32[32,128]{1,0:T(8,128)S(1)}, /*index=5*/f32[75,16384]{1,0:T(8,128)}) custom-call(s32[4,1024]{1,0:T(4,128)S(1)} %copy-done.7, s32[64,128]{1,0:T(8,128)S(1)} %bitcast.8, s32[4]{0:T(128)S(1)} %copy-done.15, ...), custom_call_target="tpu_custom_call" | custom-call | flops 1 | bytes 1 | tf_op jit(solution)/shard_map/pack_faces/pallas_call | solution.py:332
  35.8 2.6 %collective-permute-start.2 = (f32[150,1024]{1,0:T(8,128)S(1)}, f32[150,1024]{1,0:T(8,128)S(1)}, u32[]{:S(2)}, u32[]{:S(2)}) collective-permute-start(f32[150,1024]{1,0:T(8,128)S(1)} %get-tuple-element.35), channel_id=1, source_target_pairs={{0,1},{1,2},{2,3},{3,4},{4,5},{5,6},{6,7},{7,8},{8,9},{9,10},{10,1... | collective-permute-start | bytes 1843208 | tf_op jit(solution)/shard_map/ppermute | solution.py:537
  38.4 2.8 %collective-permute-start.3 = (f32[150,1024]{1,0:T(8,128)S(1)}, f32[150,1024]{1,0:T(8,128)S(1)}, u32[]{:S(2)}, u32[]{:S(2)}) collective-permute-start(f32[150,1024]{1,0:T(8,128)S(1)} %get-tuple-element.36), channel_id=1, source_target_pairs={{1,0},{2,1},{3,2},{4,3},{5,4},{6,5},{7,6},{8,7},{9,8},{10,9},{11,1... | collective-permute-start | bytes 1843208 | tf_op jit(solution)/shard_map/ppermute | solution.py:537
  41.2 4.6 %collective-permute-start = (f32[160,1024]{1,0:T(8,128)S(1)}, f32[160,1024]{1,0:T(8,128)S(1)}, u32[]{:S(2)}, u32[]{:S(2)}) collective-permute-start(f32[160,1024]{1,0:T(8,128)S(1)} %get-tuple-element.32), channel_id=1, source_target_pairs={{0,1},{1,2},{2,3},{3,4},{4,5},{5,6},{6,7},{7,8},{8,9},{9,10},{10,1... | collective-permute-start | bytes 1966088 | tf_op jit(solution)/shard_map/ppermute | solution.py:537
  45.8 6.8 %pack_sg_gx.1 = (f32[160,1024]{1,0:T(8,128)S(1)}, f32[160,1024]{1,0:T(8,128)S(1)}, f32[100,8192]{1,0:T(8,128)}, f32[60,8192]{1,0:T(8,128)}) custom-call(s32[4,1024]{1,0:T(4,128)S(1)} %copy-done.7, s32[4]{0:T(128)S(1)} %copy-done.15, f32[32,128]{1,0:T(8,128)S(1)} %get-tuple-element.37.keep, f32[100,4096]{1,0:T(8,128)S(1)} %copy-done.1, f32[60,4096]{1,0:T(8,128)S(1)} %copy-done.3), custom_call_target="tpu_custom_call" | custom-call | flops 1 | bytes 1 | tf_op jit(solution)/shard_map/pack_sg_gx/pallas_call | solution.py:158
  52.7 4.9 %collective-permute-start.4 = (f32[160,1024]{1,0:T(8,128)S(1)}, f32[160,1024]{1,0:T(8,128)S(1)}, u32[]{:S(2)}, u32[]{:S(2)}) collective-permute-start(f32[160,1024]{1,0:T(8,128)S(1)} %get-tuple-element.38), channel_id=1, source_target_pairs={{0,16},{16,32},{32,48},{48,64},{64,80},{80,96},{96,112},{1,17},{17... | collective-permute-start | bytes 1966088 | tf_op jit(solution)/shard_map/ppermute | solution.py:537
  57.6 1.9 %collective-permute-start.6 = (f32[150,1024]{1,0:T(8,128)S(1)}, f32[150,1024]{1,0:T(8,128)S(1)}, u32[]{:S(2)}, u32[]{:S(2)}) collective-permute-start(f32[150,1024]{1,0:T(8,128)S(1)} %get-tuple-element.40), channel_id=1, source_target_pairs={{0,16},{16,32},{32,48},{48,64},{64,80},{80,96},{96,112},{1,17},{17... | collective-permute-start | bytes 1843208 | tf_op jit(solution)/shard_map/ppermute | solution.py:537
  59.5 2.4 %collective-permute-start.7 = (f32[150,1024]{1,0:T(8,128)S(1)}, f32[150,1024]{1,0:T(8,128)S(1)}, u32[]{:S(2)}, u32[]{:S(2)}) collective-permute-start(f32[150,1024]{1,0:T(8,128)S(1)} %get-tuple-element.41), channel_id=1, source_target_pairs={{16,0},{32,16},{48,32},{64,48},{80,64},{96,80},{112,96},{17,1},{33... | collective-permute-start | bytes 1843208 | tf_op jit(solution)/shard_map/ppermute | solution.py:537
  62.0 1.9 %collective-permute-start.5 = (f32[160,1024]{1,0:T(8,128)S(1)}, f32[160,1024]{1,0:T(8,128)S(1)}, u32[]{:S(2)}, u32[]{:S(2)}) collective-permute-start(f32[160,1024]{1,0:T(8,128)S(1)} %get-tuple-element.39), channel_id=1, source_target_pairs={{16,0},{32,16},{48,32},{64,48},{80,64},{96,80},{112,96},{17,1},{33... | collective-permute-start | bytes 1966088 | tf_op jit(solution)/shard_map/ppermute | solution.py:537
  64.0 11.2 %pack_adj.1 = (f32[175,1024]{1,0:T(8,128)S(1)}, f32[175,1024]{1,0:T(8,128)S(1)}, f32[175,1024]{1,0:T(8,128)S(1)}, f32[175,1024]{1,0:T(8,128)S(1)}, f32[175,8192]{1,0:T(8,128)}) custom-call(s32[4,1024]{1,0:T(4,128)S(1)} %copy-done.8, s32[4]{0:T(128)S(1)} %copy-done.16, f32[32,128]{1,0:T(8,128)S(1)} %get-tuple-element.37.keep, f32[175,4096]{1,0:T(8,128)S(1)} %copy-done.4), custom_call_target="tpu_custom_call" | custom-call | flops 1 | bytes 1 | tf_op jit(solution)/shard_map/pack_adj/pallas_call | solution.py:205
  75.1 3.6 %collective-permute-start.10 = (f32[175,1024]{1,0:T(8,128)S(1)}, f32[175,1024]{1,0:T(8,128)S(1)}, u32[]{:S(2)}, u32[]{:S(2)}) collective-permute-start(f32[175,1024]{1,0:T(8,128)S(1)} %get-tuple-element.53), channel_id=1, source_target_pairs={{0,16},{16,32},{32,48},{48,64},{64,80},{80,96},{96,112},{1,17},{17... | collective-permute-start | bytes 2150408 | tf_op jit(solution)/shard_map/ppermute | solution.py:537
  78.8 1.9 %collective-permute-start.11 = (f32[175,1024]{1,0:T(8,128)S(1)}, f32[175,1024]{1,0:T(8,128)S(1)}, u32[]{:S(2)}, u32[]{:S(2)}) collective-permute-start(f32[175,1024]{1,0:T(8,128)S(1)} %get-tuple-element.54), channel_id=1, source_target_pairs={{16,0},{32,16},{48,32},{64,48},{80,64},{96,80},{112,96},{17,1},{33... | collective-permute-start | bytes 2150408 | tf_op jit(solution)/shard_map/ppermute | solution.py:537
  80.7 1.9 %collective-permute-start.8 = (f32[175,1024]{1,0:T(8,128)S(1)}, f32[175,1024]{1,0:T(8,128)S(1)}, u32[]{:S(2)}, u32[]{:S(2)}) collective-permute-start(f32[175,1024]{1,0:T(8,128)S(1)} %get-tuple-element.51), channel_id=1, source_target_pairs={{0,1},{1,2},{2,3},{3,4},{4,5},{5,6},{6,7},{7,8},{8,9},{9,10},{10,1... | collective-permute-start | bytes 2150408 | tf_op jit(solution)/shard_map/ppermute | solution.py:537
  82.7 3.4 %collective-permute-start.9 = (f32[175,1024]{1,0:T(8,128)S(1)}, f32[175,1024]{1,0:T(8,128)S(1)}, u32[]{:S(2)}, u32[]{:S(2)}) collective-permute-start(f32[175,1024]{1,0:T(8,128)S(1)} %get-tuple-element.52), channel_id=1, source_target_pairs={{1,0},{2,1},{3,2},{4,3},{5,4},{6,5},{7,6},{8,7},{9,8},{10,9},{11,1... | collective-permute-start | bytes 2150408 | tf_op jit(solution)/shard_map/ppermute | solution.py:537
  86.1 2.1 %collective-permute-start.1 = (f32[160,1024]{1,0:T(8,128)S(1)}, f32[160,1024]{1,0:T(8,128)S(1)}, u32[]{:S(2)}, u32[]{:S(2)}) collective-permute-start(f32[160,1024]{1,0:T(8,128)S(1)} %get-tuple-element.33), channel_id=1, source_target_pairs={{1,0},{2,1},{3,2},{4,3},{5,4},{6,5},{7,6},{8,7},{9,8},{10,9},{11,1... | collective-permute-start | bytes 1966088 | tf_op jit(solution)/shard_map/ppermute | solution.py:537
  88.2 10.8 %arrive_gx.1 = (f32[100,8192]{1,0:T(8,128)}, f32[60,8192]{1,0:T(8,128)}, f32[75,16384]{1,0:T(8,128)}, f32[175,4096]{1,0:T(8,128)}) custom-call(f32[3,5]{1,0:T(4,128)S(1)} %copy-done.17, f32[20,46]{1,0:T(8,128)S(1)} %bitcast.6, f32[3,20,46]{2,1,0:T(8,128)S(1)} %bitcast.4, ...), custom_call_target="tpu_custom_call", output_to_operand_aliasing={{0}: (9, {}), {1}: (10, {}), {2}: (11, {})} | custom-call | flops 1 | bytes 1 | tf_op jit(solution)/shard_map/arrive_gx/pallas_call | solution.py:477
  99.0 18.2 %collective-permute-done.1.sg_b = f32[160,1024]{1,0:T(8,128)S(1)} collective-permute-done((f32[160,1024]{1,0:T(8,128)S(1)}, f32[160,1024]{1,0:T(8,128)S(1)}, u32[]{:S(2)}, u32[]{:S(2)}) %collective-permute-start.1) | collective-permute-done | bytes 655392 | tf_op jit(solution)/shard_map/ppermute | solution.py:537
  117.2 10.8 %arrive_gy.1 = (f32[100,8192]{1,0:T(8,128)}, f32[60,8192]{1,0:T(8,128)}, f32[75,16384]{1,0:T(8,128)}, f32[175,4096]{1,0:T(8,128)}) custom-call(f32[3,5]{1,0:T(4,128)S(1)} %copy-done.17, f32[20,46]{1,0:T(8,128)S(1)} %bitcast.7, f32[3,20,46]{2,1,0:T(8,128)S(1)} %bitcast.5, ...), custom_call_target="tpu_custom_call", output_to_operand_aliasing={{0}: (9, {}), {1}: (10, {}), {2}: (11, {}), {3}: (12, {})} | custom-call | flops 1 | bytes 1 | tf_op jit(solution)/shard_map/arrive_gy/pallas_call | solution.py:477
  128.0 1.1 place_gx.1.ad_in
  129.2 1.1 place_gy.1
  (44 shorter events, 3.6 us)
Async XLA Ops:
  0.6 1.5 %copy-start = (f32[100,4096]{1,0:T(8,128)S(1)}, f32[100,4096]{1,0:T(8,128)}, u32[]{:S(2)}) copy-start(f32[100,4096]{1,0:T(8,128)} %st.3) | copy-start | bytes 4915204
  4.7 41.1 %copy-start.1 = (f32[100,4096]{1,0:T(8,128)S(1)}, f32[100,4096]{1,0:T(8,128)}, u32[]{:S(2)}) copy-start(f32[100,4096]{1,0:T(8,128)} %st.3) | copy-start | bytes 4915204
  4.7 41.1 %copy-start.3 = (f32[60,4096]{1,0:T(8,128)S(1)}, f32[60,4096]{1,0:T(8,128)}, u32[]{:S(2)}) copy-start(f32[60,4096]{1,0:T(8,128)} %ge.3) | copy-start | bytes 2949124
  4.7 59.3 %copy-start.8 = (s32[4,1024]{1,0:T(4,128)S(1)}, s32[4,1024]{1,0:T(4,128)}, u32[]{:S(2)}) copy-start(s32[4,1024]{1,0:T(4,128)} %ids_v.7) | copy-start | bytes 49156
  4.7 59.3 %copy-start.16 = (s32[4]{0:T(128)S(1)}, s32[4]{0:T(128)}, u32[]{:S(2)}) copy-start(s32[4]{0:T(128)} %cnt.7) | copy-start | bytes 52
  11.5 52.5 %copy-start.4 = (f32[175,4096]{1,0:T(8,128)S(1)}, f32[175,4096]{1,0:T(8,128)}, u32[]{:S(2)}) copy-start(f32[175,4096]{1,0:T(8,128)} %ad) | copy-start | bytes 8601604
  11.5 1.9 %copy-start.5 = (f32[75,8192]{1,0:T(8,128)S(1)}, f32[75,8192]{1,0:T(8,128)}, u32[]{:S(2)}) copy-start(f32[75,8192]{1,0:T(8,128)} %fb) | copy-start | bytes 7372804
  35.7 52.5 %copy-start.9 = (f32[35,138]{1,0:T(8,128)S(1)}, f32[35,138]{1,0:T(8,128)}, u32[]{:S(2)}) copy-start(f32[35,138]{1,0:T(8,128)} %test.3) | copy-start | bytes 57964
  35.7 52.4 %copy-start.10 = (f32[3,46,20]{1,2,0:T(8,128)S(1)}, f32[3,46,20]{1,2,0:T(8,128)}, u32[]{:S(2)}) copy-start(f32[3,46,20]{1,2,0:T(8,128)} %param.20) | copy-start | bytes 33124
  35.7 52.4 %copy-start.11 = (f32[46,20]{0,1:T(8,128)S(1)}, f32[46,20]{0,1:T(8,128)}, u32[]{:S(2)}) copy-start(f32[46,20]{0,1:T(8,128)} %param.19) | copy-start | bytes 11044
  35.8 52.4 %copy-start.13 = (f32[35,15]{0,1:T(8,128)S(1)}, f32[35,15]{0,1:T(8,128)}, u32[]{:S(2)}) copy-start(f32[35,15]{0,1:T(8,128)} %param.22) | copy-start | bytes 6304
  35.8 52.4 %copy-start.17 = (f32[3,5]{1,0:T(4,128)S(1)}, f32[3,5]{1,0:T(4,128)}, u32[]{:S(2)}) copy-start(f32[3,5]{1,0:T(4,128)} %speeds.3) | copy-start | bytes 184
  35.8 23.8 %collective-permute-start.2 = (f32[150,1024]{1,0:T(8,128)S(1)}, f32[150,1024]{1,0:T(8,128)S(1)}, u32[]{:S(2)}, u32[]{:S(2)}) collective-permute-start(f32[150,1024]{1,0:T(8,128)S(1)} %get-tuple-element.35), channel_id=1, source_target_pairs={{0,1},{1,2},{2,3},{3,4},{4,5},{5,6},{6,7},{7,8},{8,9},{9,10},{10,1... | collective-permute-start | bytes 1843208 | tf_op jit(solution)/shard_map/ppermute | solution.py:537
  38.4 23.6 %collective-permute-start.3 = (f32[150,1024]{1,0:T(8,128)S(1)}, f32[150,1024]{1,0:T(8,128)S(1)}, u32[]{:S(2)}, u32[]{:S(2)}) collective-permute-start(f32[150,1024]{1,0:T(8,128)S(1)} %get-tuple-element.36), channel_id=1, source_target_pairs={{1,0},{2,1},{3,2},{4,3},{5,4},{6,5},{7,6},{8,7},{9,8},{10,9},{11,1... | collective-permute-start | bytes 1843208 | tf_op jit(solution)/shard_map/ppermute | solution.py:537
  41.2 39.5 %collective-permute-start = (f32[160,1024]{1,0:T(8,128)S(1)}, f32[160,1024]{1,0:T(8,128)S(1)}, u32[]{:S(2)}, u32[]{:S(2)}) collective-permute-start(f32[160,1024]{1,0:T(8,128)S(1)} %get-tuple-element.32), channel_id=1, source_target_pairs={{0,1},{1,2},{2,3},{3,4},{4,5},{5,6},{6,7},{7,8},{8,9},{9,10},{10,1... | collective-permute-start | bytes 1966088 | tf_op jit(solution)/shard_map/ppermute | solution.py:537
  52.7 30.0 %collective-permute-start.4 = (f32[160,1024]{1,0:T(8,128)S(1)}, f32[160,1024]{1,0:T(8,128)S(1)}, u32[]{:S(2)}, u32[]{:S(2)}) collective-permute-start(f32[160,1024]{1,0:T(8,128)S(1)} %get-tuple-element.38), channel_id=1, source_target_pairs={{0,16},{16,32},{32,48},{48,64},{64,80},{80,96},{96,112},{1,17},{17... | collective-permute-start | bytes 1966088 | tf_op jit(solution)/shard_map/ppermute | solution.py:537
  57.6 17.5 %collective-permute-start.6 = (f32[150,1024]{1,0:T(8,128)S(1)}, f32[150,1024]{1,0:T(8,128)S(1)}, u32[]{:S(2)}, u32[]{:S(2)}) collective-permute-start(f32[150,1024]{1,0:T(8,128)S(1)} %get-tuple-element.40), channel_id=1, source_target_pairs={{0,16},{16,32},{32,48},{48,64},{64,80},{80,96},{96,112},{1,17},{17... | collective-permute-start | bytes 1843208 | tf_op jit(solution)/shard_map/ppermute | solution.py:537
  59.5 19.2 %collective-permute-start.7 = (f32[150,1024]{1,0:T(8,128)S(1)}, f32[150,1024]{1,0:T(8,128)S(1)}, u32[]{:S(2)}, u32[]{:S(2)}) collective-permute-start(f32[150,1024]{1,0:T(8,128)S(1)} %get-tuple-element.41), channel_id=1, source_target_pairs={{16,0},{32,16},{48,32},{64,48},{80,64},{96,80},{112,96},{17,1},{33... | collective-permute-start | bytes 1843208 | tf_op jit(solution)/shard_map/ppermute | solution.py:537
  62.0 24.0 %collective-permute-start.5 = (f32[160,1024]{1,0:T(8,128)S(1)}, f32[160,1024]{1,0:T(8,128)S(1)}, u32[]{:S(2)}, u32[]{:S(2)}) collective-permute-start(f32[160,1024]{1,0:T(8,128)S(1)} %get-tuple-element.39), channel_id=1, source_target_pairs={{16,0},{32,16},{48,32},{64,48},{80,64},{96,80},{112,96},{17,1},{33... | collective-permute-start | bytes 1966088 | tf_op jit(solution)/shard_map/ppermute | solution.py:537
  75.1 52.9 %collective-permute-start.10 = (f32[175,1024]{1,0:T(8,128)S(1)}, f32[175,1024]{1,0:T(8,128)S(1)}, u32[]{:S(2)}, u32[]{:S(2)}) collective-permute-start(f32[175,1024]{1,0:T(8,128)S(1)} %get-tuple-element.53), channel_id=1, source_target_pairs={{0,16},{16,32},{32,48},{48,64},{64,80},{80,96},{96,112},{1,17},{17... | collective-permute-start | bytes 2150408 | tf_op jit(solution)/shard_map/ppermute | solution.py:537
  78.8 49.2 %collective-permute-start.11 = (f32[175,1024]{1,0:T(8,128)S(1)}, f32[175,1024]{1,0:T(8,128)S(1)}, u32[]{:S(2)}, u32[]{:S(2)}) collective-permute-start(f32[175,1024]{1,0:T(8,128)S(1)} %get-tuple-element.54), channel_id=1, source_target_pairs={{16,0},{32,16},{48,32},{64,48},{80,64},{96,80},{112,96},{17,1},{33... | collective-permute-start | bytes 2150408 | tf_op jit(solution)/shard_map/ppermute | solution.py:537
  80.7 48.4 %collective-permute-start.8 = (f32[175,1024]{1,0:T(8,128)S(1)}, f32[175,1024]{1,0:T(8,128)S(1)}, u32[]{:S(2)}, u32[]{:S(2)}) collective-permute-start(f32[175,1024]{1,0:T(8,128)S(1)} %get-tuple-element.51), channel_id=1, source_target_pairs={{0,1},{1,2},{2,3},{3,4},{4,5},{5,6},{6,7},{7,8},{8,9},{9,10},{10,1... | collective-permute-start | bytes 2150408 | tf_op jit(solution)/shard_map/ppermute | solution.py:537
  82.7 46.5 %collective-permute-start.9 = (f32[175,1024]{1,0:T(8,128)S(1)}, f32[175,1024]{1,0:T(8,128)S(1)}, u32[]{:S(2)}, u32[]{:S(2)}) collective-permute-start(f32[175,1024]{1,0:T(8,128)S(1)} %get-tuple-element.52), channel_id=1, source_target_pairs={{1,0},{2,1},{3,2},{4,3},{5,4},{6,5},{7,6},{8,7},{9,8},{10,9},{11,1... | collective-permute-start | bytes 2150408 | tf_op jit(solution)/shard_map/ppermute | solution.py:537
  86.1 31.2 %collective-permute-start.1 = (f32[160,1024]{1,0:T(8,128)S(1)}, f32[160,1024]{1,0:T(8,128)S(1)}, u32[]{:S(2)}, u32[]{:S(2)}) collective-permute-start(f32[160,1024]{1,0:T(8,128)S(1)} %get-tuple-element.33), channel_id=1, source_target_pairs={{1,0},{2,1},{3,2},{4,3},{5,4},{6,5},{7,6},{8,7},{9,8},{10,9},{11,1... | collective-permute-start | bytes 1966088 | tf_op jit(solution)/shard_map/ppermute | solution.py:537
  (6 other events, 4.7 us)
